TPU v7x, 256 devices: a whole 4x4x8 slice. The times are simulated.
256 devices in a mesh: dp: 2 (over z_lo), seq: 32 (over y, x, core), head: 4 (over z_hi).
Axes of the slice: x: 4, y: 4, z: 8 (z_hi: 4, z_lo: 2; z = z_hi * 2 + z_lo), core: 2. Of those that a mesh axis runs over, the one named last changes fastest.
Arguments:
- x_in: bfloat16 [2, 24576, 4096], P('dp', 'seq', 'head'), may hold values from -6 to 6
- b_in: bfloat16 [2, 24576, 1024], P('dp', 'seq', 'head'), may hold values from -6 to 6
- c_in: bfloat16 [2, 24576, 1024], P('dp', 'seq', 'head'), may hold values from -6 to 6
- z_in: bfloat16 [2, 24576, 4096], P('dp', 'seq', 'head'), may hold values from -24 to 24
- dt_in: float32 [2, 64, 24576], P('dp', 'head', 'seq'), may hold values from -10 to 4.5
- a_log: float32 [64], P('head'), may hold values from -2.3 to 0.58
- skip_gain: float32 [64], P('head'), may hold values from 0.5 to 1.5
- norm_gain: float32 [4096], P('head'), may hold values from 0.5 to 1.5
- conv_x: float32 [4, 4096], P(None, 'head'), may hold values from -3 to 3
- conv_b: float32 [4, 1024], P(None, 'head'), may hold values from -3 to 3
- conv_c: float32 [4, 1024], P(None, 'head'), may hold values from -3 to 3
- init_state: float32 [2, 64, 64, 128], P('dp', 'head'), may hold values from -0.5 to 0.5
- out_weight: bfloat16 [4096, 8192], P(('dp', 'seq'), 'head'), may hold values from -0.09375 to 0.09375
Outputs:
- mixed: bfloat16 [2, 24576, 8192], P('dp', 'seq', 'head')
All inputs are finite; a program needn't handle non-finite values.
Results may differ from a plain program's by a relative error of at most 0.0058.
Values may be sent and summed in bfloat16 or wider, within the bound.
No kernel may reach another device: no remote copies, remote signals or barrier semaphores. Data moves between devices by JAX's collectives and lax.ppermute only.
A program may use at most 128 MiB of HBM per device.

v0:
```python
import jax
import jax.numpy as jnp
from jax import lax
from jax.sharding import PartitionSpec as P

HEAD_SIZE = 64
STATE = 128
BLOCK_LEN = 256
TAPS = 4


EPSILON = 1e-05


def from_behind(block, axis, distance):
    devices = range(lax.axis_size(axis))
    route = [(i - distance, i) for i in devices if i - distance in devices]
    return lax.ppermute(block, axis, route)


def entering(value, axis, join, neutral):
    count, mine = (lax.axis_size(axis), lax.axis_index(axis))
    pieces = jax.tree.map(lambda part: lax.all_gather(part, axis), value)
    subtotal = jax.tree.map(
        lambda part, zero: jnp.full_like(part, 0) + jnp.asarray(zero, part.dtype), value, neutral
    )

    def step(position, subtotal):
        longer = join(subtotal, jax.tree.map(lambda part: part[position], pieces))
        return jax.tree.map(lambda new, old: jnp.where(position < mine, new, old), longer, subtotal)

    return lax.fori_loop(0, count - 1, step, subtotal)


def causal_conv(signal, before, weight):
    joined = jnp.concatenate([before, signal], axis=1).astype(jnp.float32)
    length = signal.shape[1]
    tap_count = weight.shape[0]
    accum_total = weight[0] * joined[:, 0:length]
    for offset in range(1, tap_count):
        accum_total = accum_total + weight[offset] * joined[:, offset : offset + length]
    return jax.nn.silu(accum_total).astype(jnp.bfloat16)


def combine_states(first_pair, second_pair):
    return (
        first_pair[0] * second_pair[0],
        second_pair[0][..., None, None] * first_pair[1] + second_pair[1],
    )


def local(
    x_in,
    b_in,
    c_in,
    z_in,
    dt_in,
    a_log,
    skip_gain,
    norm_gain,
    conv_x,
    conv_b,
    conv_c,
    init_state,
    out_weight,
):
    highest = lax.Precision.HIGHEST
    roll_count, tok_count, wide_x = x_in.shape
    wide_b = b_in.shape[2]
    head_count = dt_in.shape[1]
    group_count = wide_b // STATE
    per_group = head_count // group_count
    block_count = tok_count // BLOCK_LEN
    rim_width = TAPS - 1
    edge_rows = jnp.concatenate(
        [
            x_in[:, tok_count - rim_width :],
            b_in[:, tok_count - rim_width :],
            c_in[:, tok_count - rim_width :],
        ],
        axis=2,
    )
    before = from_behind(edge_rows, "seq", 1)
    x_conv = causal_conv(x_in, before[:, :, :wide_x], conv_x)
    b_conv = causal_conv(b_in, before[:, :, wide_x : wide_x + wide_b], conv_b)
    c_conv = causal_conv(c_in, before[:, :, wide_x + wide_b :], conv_c)
    grouped = (roll_count, group_count, per_group, block_count, BLOCK_LEN)
    step_flat = jax.nn.softplus(dt_in)
    decay_rate = -jnp.exp(a_log)
    cum_decay = jnp.cumsum((step_flat * decay_rate[None, :, None]).reshape(grouped), axis=-1)
    step_size = step_flat.reshape(grouped)
    x_shaped = x_conv.reshape(roll_count, block_count, BLOCK_LEN, group_count, per_group, HEAD_SIZE)
    b_shaped = b_conv.reshape(roll_count, block_count, BLOCK_LEN, group_count, STATE)
    c_shaped = c_conv.reshape(roll_count, block_count, BLOCK_LEN, group_count, STATE)
    scores = jnp.einsum(
        "rcqgn,rcsgn->rgcqs", c_shaped, b_shaped, preferred_element_type=jnp.float32
    )
    query_pos = lax.broadcasted_iota(jnp.int32, (BLOCK_LEN, BLOCK_LEN), 0)
    key_pos = lax.broadcasted_iota(jnp.int32, (BLOCK_LEN, BLOCK_LEN), 1)
    causal = query_pos >= key_pos
    spread = cum_decay[..., :, None] - cum_decay[..., None, :]
    decay_mat = jnp.where(causal, jnp.exp(jnp.minimum(spread, 0.0)), jnp.float32(0.0))
    mixing = (scores[:, :, None] * decay_mat * step_size[..., None, :]).astype(jnp.bfloat16)
    intra_out = jnp.einsum(
        "rgkcqs,rcsgkp->rcqgkp", mixing, x_shaped, preferred_element_type=jnp.float32
    )
    last_decay = cum_decay[..., -1:]
    weights_in = jnp.exp(last_decay - cum_decay) * step_size
    weighted = (
        jnp.transpose(weights_in, (0, 3, 4, 1, 2))[..., None] * x_shaped.astype(jnp.float32)
    ).astype(jnp.bfloat16)
    block_states = jnp.einsum(
        "rcsgkp,rcsgn->rgkcpn", weighted, b_shaped, preferred_element_type=jnp.float32
    )
    block_decay = jnp.exp(last_decay[..., 0])
    running = jnp.zeros((roll_count, group_count, per_group, HEAD_SIZE, STATE), jnp.float32)
    carried = jnp.ones((roll_count, group_count, per_group), jnp.float32)
    starts = []
    factors = []
    for block_index in range(block_count):
        starts.append(running)
        factors.append(carried)
        running = (
            block_decay[..., block_index, None, None] * running + block_states[:, :, :, block_index]
        )
        carried = carried * block_decay[..., block_index]
    prefix_decay, prefix_state = entering(
        (carried, running), "seq", combine_states, (jnp.ones_like(carried), jnp.zeros_like(running))
    )
    incoming = prefix_state + prefix_decay[..., None, None] * init_state.reshape(
        roll_count, group_count, per_group, HEAD_SIZE, STATE
    )
    start_states = jnp.stack(
        [
            factors[block_index][..., None, None] * incoming + starts[block_index]
            for block_index in range(block_count)
        ],
        axis=3,
    )
    c_float = c_shaped.astype(jnp.float32)
    inter_out = jnp.einsum("rcqgn,rgkcpn->rcqgkp", c_float, start_states, precision=highest)
    inter_out = inter_out * jnp.transpose(jnp.exp(cum_decay), (0, 3, 4, 1, 2))[..., None]
    skip_shaped = skip_gain.reshape(group_count, per_group)[:, :, None]
    ssm_out = (intra_out + inter_out + skip_shaped * x_shaped.astype(jnp.float32)).reshape(
        roll_count, tok_count, group_count, per_group * HEAD_SIZE
    )
    gate_act = jax.nn.silu(z_in.astype(jnp.float32)).reshape(
        roll_count, tok_count, group_count, per_group * HEAD_SIZE
    )
    gated_out = ssm_out * gate_act
    mean_sq = jnp.mean(gated_out * gated_out, axis=-1, keepdims=True)
    normed = (
        gated_out
        * lax.rsqrt(mean_sq + EPSILON)
        * norm_gain.reshape(group_count, per_group * HEAD_SIZE)
    )
    normed = normed.astype(jnp.bfloat16).reshape(roll_count * tok_count, wide_x)
    wide_all = lax.all_gather(normed, "head", axis=1, tiled=True)
    full_weight = lax.all_gather(out_weight, ("dp", "seq"), axis=0, tiled=True)
    mixed_terms = jnp.dot(wide_all, full_weight, preferred_element_type=jnp.float32)
    return mixed_terms.astype(jnp.bfloat16).reshape(roll_count, tok_count, -1)


def solution(mesh):
    in_specs = (
        P("dp", "seq", "head"),
        P("dp", "seq", "head"),
        P("dp", "seq", "head"),
        P("dp", "seq", "head"),
        P("dp", "head", "seq"),
        P("head"),
        P("head"),
        P("head"),
        P(None, "head"),
        P(None, "head"),
        P(None, "head"),
        P("dp", "head", None, None),
        P(("dp", "seq"), "head"),
    )
    out_specs = P("dp", "seq", "head")
    return jax.shard_map(local, mesh=mesh, in_specs=in_specs, out_specs=out_specs, check_vma=False)
```

profile of v0, /device:TPU:65, one launch (start us, length us, event | category | flops | bytes accessed | tf_op | source)
XLA Modules:
  0.0 390.5 jit_solution(8210310024297503800)
XLA Ops:
  9.6 3.7 collective-permute-start
  14.9 3.4 reduce-window.6
  22.2 1.7 copy.154
  26.1 3.5 multiply_convert_fusion.3
  29.7 2.1 reshape.545
  33.5 2.6 multiply_convert_fusion.2
  38.9 2.6 copy.182
  41.5 3.9 convert_multiply_fusion
  45.5 5.9 %reshape.560 = f32[1,3,256,2,8,64]{2,1,5,4,3,0:T(4,128)} reshape(f32[1,768,1024]{1,2,0:T(8,128)} %convert_multiply_fusion) | data formatting | bytes 6291456 | tf_op jit(solution)/shard_map/reshape | solution.py:147
  52.1 25.1 %all-gather = f32[32,2,8,1]{2,1,3,0:T(2,128)} all-gather(f32[1,2,8,1]{2,1,3,0:T(2,128)S(1)} %copy-done.18), channel_id=2, replica_groups=mesh['dp'=2,'seq'=32,'head'=4] {'seq'}, dimensions={0}, use_global_device_ids=true | all-gather | bytes 2112 | tf_op jit(solution)/shard_map/all_gather | solution.py:23
  78.5 5.7 %reshape.562 = f32[1,3,256,2,8,64]{2,1,5,4,3,0:T(4,128)} reshape(bf16[1,768,1024]{1,2,0:T(8,128)(2,1)} %copy-done.1) | data formatting | bytes 4718592 | tf_op jit(solution)/shard_map/convert_element_type | solution.py:110
  84.4 1.2 multiply_convert_fusion.5
  85.7 1.6 fusion.44
  87.2 7.5 %fusion.1 = f32[3,2,8,64,256]{4,3,2,1,0:T(8,128)} fusion(f32[2,3,256,256]{3,2,0,1:T(8,128)} %fusion.44, pred[256,256]{1,0:T(8,128)(4,1)S(1)} %iota_compare_fusion, bf16[3,256,2,8,64]{1,0,4,3,2:T(4,128)(2,1)} %reshape.545, f32[2,8,3,256]{3,1,2,0:T(8,128)S(1)} %bitcast.161, f32[2,8,3,256]{3,1,2,0:T(8,128)S(1)} %copy-done.8), kind=kOutput, calls=%fused_computation.5 | convolution fusion | flops 421527552 | bytes 6455296 | tf_op jit(solution)/shard_map/rgkcqs,rcsgkp->rcqgkp/dot_general | solution.py:104
  94.7 22.5 %all-gather.5.cloned.1.call-done = f32[32,1,2,8,64,128]{5,4,3,2,1,0:T(8,128)} async-done(((f32[1,1,2,8,64,128]{5,4,3,2,1,0:T(8,128)}), f32[32,1,2,8,64,128]{5,4,3,2,1,0:T(8,128)}) %all-gather.5.cloned.1.call-update) | async-done | bytes 16777232 | tf_op jit(solution)/shard_map/all_gather | solution.py:23
  117.3 78.2 %while.16 = (s32[]{:T(128)}, f32[1,2,8]{2,1,0:T(2,128)S(1)}, f32[1,2,8,64,128]{4,3,2,1,0:T(8,128)S(1)}, s32[]{:T(128)}, f32[32,1,2,8]{3,2,1,0:T(2,128)}, /*index...) while((s32[]{:T(128)}, f32[1,2,8]{2,1,0:T(2,128)S(1)}, ...), condition=%wide.region_3.4_spmd.clone, body=%wide.region_2.3_spmd.clone.sunk | while | flops 524340 | bytes 1573367 | solution.py:32
  118.0 1.2 fusion.59
  120.6 1.2 fusion.59
  123.1 1.2 fusion.59
  125.6 1.2 fusion.59
  128.1 1.2 fusion.59
  130.6 1.2 fusion.59
  135.6 1.2 fusion.59
  140.6 1.2 fusion.59
  143.1 1.2 fusion.59
  148.2 1.2 fusion.59
  150.7 1.2 fusion.59
  153.2 1.2 fusion.59
  155.8 1.2 fusion.59
  158.3 1.2 fusion.59
  160.8 1.2 fusion.59
  163.3 1.2 fusion.59
  165.8 1.2 fusion.59
  173.4 1.2 fusion.59
  175.9 1.2 fusion.59
  178.4 1.2 fusion.59
  180.9 1.2 fusion.59
  183.5 1.2 fusion.59
  186.0 1.2 fusion.59
  188.5 1.2 fusion.59
  191.1 1.2 fusion.59
  195.9 1.8 copy-done.2
  197.7 4.8 %fusion.19 = (f32[3,256,2]{1,2,0:T(2,128)S(1)}, f32[1,3,256,2,8,64]{2,5,4,3,1,0:T(8,128)S(1)}) fusion(f32[1,3,256,2,8,64]{2,1,5,4,3,0:T(4,128)S(1)} %copy-done.2, f32[1,3,256,2,8,64]{2,1,5,4,3,0:T(4,128)} %reshape.562, f32[2,8]{1,0:T(2,128)S(1)} %copy-done.15, f32[3,256,2,8]{1,3,2,0:T(8,128)S(1)} %bitcast.163, ...), kind=kOutput, calls=%fused_computation.35 | convolution fusion | flops 1214249472 | bytes 14604352 | tf_op jit(solution)/shard_map/rcqgn,rgkcpn->rcqgkp/dot_general | solution.py:141
  202.5 2.2 copy.181
  206.1 2.2 fusion.17
  208.4 34.6 %all-gather.9.cloned.1.call-done = bf16[4096,2048]{1,0:T(8,128)(2,1)} async-done(((bf16[64,2048]{1,0:T(8,128)(2,1)}), bf16[4096,2048]{1,0:T(8,128)(2,1)}) %all-gather.9.cloned.1.call-update) | async-done | bytes 16777232 | tf_op jit(solution)/shard_map/all_gather | solution.py:159
  243.0 121.2 %all-gather.7.cloned.1.call-done = bf16[768,4096]{0,1:T(8,128)(2,1)} async-done(((bf16[768,1024]{0,1:T(8,128)(2,1)}), bf16[768,4096]{0,1:T(8,128)(2,1)}) %all-gather.7.cloned.1.call-update) | async-done | bytes 6291472 | tf_op jit(solution)/shard_map/all_gather | solution.py:158
  364.2 19.8 %fusion.20 = bf16[1,768,2048]{2,1,0:T(8,128)(2,1)} fusion(bf16[768,4096]{0,1:T(8,128)(2,1)} %all-gather.7.cloned.1.call-done, bf16[4096,2048]{1,0:T(8,128)(2,1)} %all-gather.9.cloned.1.call-done), kind=kOutput, calls=%fused_computation.38 | convolution fusion | flops 12886474752 | bytes 26214400 | tf_op jit(solution)/shard_map/dot_general | solution.py:160
  (171 shorter events, 67.7 us)
Async XLA Ops:
  6.5 110.7 %all-gather.5.cloned.1.call-start = ((), (), s32[]{:S(2)}) async-start(), calls=%async_computation | async-start | bytes 17301504 | tf_op jit(solution)/shard_map/all_gather | solution.py:23
  9.6 14.8 %collective-permute-start = (bf16[1,3,1536]{1,2,0:T(8,128)(2,1)}, bf16[1,3,1536]{1,2,0:T(8,128)(2,1)}, u32[]{:S(2)}, u32[]{:S(2)}) collective-permute-start(bf16[1,3,1536]{1,2,0:T(8,128)(2,1)} %copy.153), channel_id=1, source_target_pairs={{0,4},{4,8},{8,12},{12,16},{16,20},{20,24},{24,28},{28,32},{32,36}... | collective-permute-start | bytes 27656 | tf_op jit(solution)/shard_map/ppermute | solution.py:18
  14.8 5.7 %copy-start.12 = (f32[4,1024]{1,0:T(4,128)S(1)}, f32[4,1024]{1,0:T(4,128)}, u32[]{:S(2)}) copy-start(f32[4,1024]{1,0:T(4,128)} %param.23) | copy-start | bytes 49156
  14.8 5.7 %copy-start.19 = (f32[4,256]{1,0:T(4,128)S(1)}, f32[4,256]{1,0:T(4,128)}, u32[]{:S(2)}) copy-start(f32[4,256]{1,0:T(4,128)} %param.24) | copy-start | bytes 12292
  18.6 3.1 copy-start.6
  21.1 15.5 %copy-start.13 = (f32[2,8]{1,0:T(2,128)}, f32[2,8]{1,0:T(2,128)S(1)}, u32[]{:S(2)}) copy-start(f32[2,8]{1,0:T(2,128)S(1)} %get-tuple-element.212) | copy-start | bytes 196
  22.2 14.4 %copy-start.10 = (f32[2,8]{1,0:T(2,128)}, f32[2,8]{1,0:T(2,128)S(1)}, u32[]{:S(2)}) copy-start(f32[2,8]{1,0:T(2,128)S(1)} %get-tuple-element.209) | copy-start | bytes 196
  29.6 3.7 copy-start.1
  29.7 3.1 copy-start.4
  37.7 205.3 %all-gather.9.cloned.1.call-start = ((), (), s32[]{:S(2)}) async-start(), calls=%async_computation.2 | async-start | bytes 17039360 | tf_op jit(solution)/shard_map/all_gather | solution.py:159
  38.5 325.7 %all-gather.7.cloned.1.call-start = ((), (), s32[]{:S(2)}) async-start(), calls=%async_computation.1 | async-start | bytes 7864320 | tf_op jit(solution)/shard_map/all_gather | solution.py:158
  45.4 6.0 %copy-start.22 = (f32[16]{0:T(128)S(1)}, f32[16]{0:T(128)}, u32[]{:S(2)}) copy-start(f32[16]{0:T(128)} %param.21) | copy-start | bytes 196
  45.4 6.6 %copy-start.18 = (f32[1,2,8,1]{2,1,3,0:T(2,128)S(1)}, f32[1,2,8,1]{2,1,3,0:T(2,128)}, u32[]{:S(2)}) copy-start(f32[1,2,8,1]{2,1,3,0:T(2,128)} %get-tuple-element.211) | copy-start | bytes 196
  45.4 31.7 %copy-start.20 = (f32[4,256]{1,0:T(4,128)S(1)}, f32[4,256]{1,0:T(4,128)}, u32[]{:S(2)}) copy-start(f32[4,256]{1,0:T(4,128)} %param.25) | copy-start | bytes 12292
  45.4 32.3 %copy-start.7 = (f32[2,8,3,2]{1,3,2,0:T(2,128)S(1)}, f32[2,8,3,2]{1,3,2,0:T(2,128)}, u32[]{:S(2)}) copy-start(f32[2,8,3,2]{1,3,2,0:T(2,128)} %copy-done.6) | copy-start | bytes 1156
  51.4 32.9 %copy-start.5 = (bf16[1,768,256]{2,1,0:T(8,128)(2,1)S(1)}, bf16[1,768,256]{2,1,0:T(8,128)(2,1)}, u32[]{:S(2)}) copy-start(bf16[1,768,256]{2,1,0:T(8,128)(2,1)} %param.17) | copy-start | bytes 1179652
  84.4 2.9 copy-start.8
  87.2 30.0 %copy-start.9 = (f32[1,2,8]{2,1,0:T(2,128)S(1)}, f32[1,2,8]{2,1,0:T(2,128)}, u32[]{:S(2)}) copy-start(f32[1,2,8]{2,1,0:T(2,128)} %custom-call) | copy-start | bytes 196
  117.3 78.2 %copy-start.3 = (f32[1,16,64,128]{3,2,1,0:T(8,128)S(1)}, f32[1,16,64,128]{3,2,1,0:T(8,128)}, u32[]{:S(2)}) copy-start(f32[1,16,64,128]{3,2,1,0:T(8,128)} %param.26) | copy-start | bytes 1572868
  117.3 78.2 %copy-start.11 = (f32[2,8]{1,0:T(2,128)S(1)}, f32[2,8]{1,0:T(2,128)}, u32[]{:S(2)}) copy-start(f32[2,8]{1,0:T(2,128)} %copy-done.10) | copy-start | bytes 196
  117.3 78.2 %copy-start.16 = (f32[2,8]{1,0:T(2,128)S(1)}, f32[2,8]{1,0:T(2,128)}, u32[]{:S(2)}) copy-start(f32[2,8]{1,0:T(2,128)} %get-tuple-element.213) | copy-start | bytes 196
  117.3 78.4 %copy-start.14 = (f32[2,8]{1,0:T(2,128)S(1)}, f32[2,8]{1,0:T(2,128)}, u32[]{:S(2)}) copy-start(f32[2,8]{1,0:T(2,128)} %copy-done.13) | copy-start | bytes 196
  117.3 78.4 %copy-start.17 = (f32[2,8]{1,0:T(2,128)S(1)}, f32[2,8]{1,0:T(2,128)}, u32[]{:S(2)}) copy-start(f32[2,8]{1,0:T(2,128)} %get-tuple-element.208) | copy-start | bytes 196
  195.5 2.3 copy-start.2
  195.5 2.3 copy-start.15
  204.7 1.4 copy-start
  204.7 1.4 copy-start.21
Sparse Core Ops, SparseCore 0:
  37.8 79.3 all-gather.4
  119.1 123.8 all-gather.8
  244.8 119.2 all-gather.6
where the time goes:
time: 394 us; the launch traced here: 390 us
  waiting for transfers between devices  179 us (45%)
  other arithmetic  81.8 us (21%)
  local copies, waits for them, and re-layouts  53 us (13%)
  matrix products  34.2 us (9%)
  blocking collectives  25.1 us (6%)
  between operations  13.6 us (3%)
    all_gather x1, waiting for transfers between devices, local(): wide_all = lax.all_gather(normed, 'head', axis=1, tiled=True)  121 us
    select_n x62, other arithmetic, step(): jnp.where(position < mine, new, old)  57.5 us
    all_gather x1, waiting for transfers between devices, local(): full_weight = lax.all_gather(out_weight, ('dp', 'seq'), axis=0, tiled=True)  34.6 us
    all_gather x1, blocking collectives, entering(): pieces = jax.tree.map(lambda part: lax.all_gather(part, axis), value)  25.1 us
    all_gather x1, waiting for transfers between devices, entering(): pieces = jax.tree.map(lambda part: lax.all_gather(part, axis), value)  22.5 us
    mul x31, local copies, waits for them, and re-layouts, combine_states(): second_pair[0][..., None, None] * first_pair[1] + second_pair[1]  20.5 us
    dot_general x1, matrix products, local(): jnp.dot(wide_all, full_weight, preferred_element_type=jnp.float32)  19.8 us
  transfers between devices with their start and end apart: 4, of which 3 were waited for; matrix products, arithmetic and copies ran while one was open for 33% of the time, Pallas kernels for 0%

commit v1 on v0

v1 whole, which is shorter than its diff:
```python
import math

import jax
import jax.numpy as jnp
from jax import lax
from jax.experimental import pallas as pl
from jax.experimental.pallas import tpu as pltpu
from jax.sharding import PartitionSpec as P

HEAD_SIZE = 64
STATE = 128
TAPS = 4
SUB = 128
CHUNK = 256
EPSILON = 1e-05
LOG2E = math.log2(math.e)
F32 = jnp.float32
BF16 = jnp.bfloat16


def dot(a, b, dims=((1,), (0,))):
    return lax.dot_general(a, b, (dims, ((), ())), preferred_element_type=F32)


def silu(v):
    half = 0.5 * v
    return half + half * jnp.tanh(half)


def split_two(v):
    high = v.astype(BF16)
    low = (v - high.astype(F32)).astype(BF16)
    return high, low


def head_of_lane(heads, width):
    lane = lax.broadcasted_iota(jnp.int32, (heads, width), 1)
    row = lax.broadcasted_iota(jnp.int32, (heads, width), 0)
    return lane // HEAD_SIZE == row


def widen_row(column, width):
    mask = head_of_lane(column.shape[0], width)
    return jnp.sum(jnp.where(mask, column, 0.0), axis=0, keepdims=True)


def column_of(ref, heads):
    row = lax.broadcasted_iota(jnp.int32, (heads, 1), 0)
    column = jnp.zeros((heads, 1), F32)
    for h in range(heads):
        column = jnp.where(row == h, ref[h], column)
    return column


def widen_tokens(rows, width):
    heads = rows.shape[0]
    mask = head_of_lane(heads, width).astype(F32).astype(BF16)
    high, low = split_two(rows)
    return dot(
        jnp.concatenate([high, low], axis=0), jnp.concatenate([mask, mask], axis=0), ((0,), (0,))
    )


def edge_kernel(x_ref, b_ref, c_ref, out_ref):
    wide_x, wide_b = x_ref.shape[1], b_ref.shape[1]
    out_ref[:, :wide_x] = x_ref[...]
    out_ref[:, wide_x : wide_x + wide_b] = b_ref[...]
    out_ref[:, wide_x + wide_b :] = c_ref[...]


def edge_rows(x, b, c):
    tokens, wide_x = x.shape
    wide_b = b.shape[1]
    last = tokens // 8 - 1
    return pl.pallas_call(
        edge_kernel,
        grid=(1,),
        in_specs=[
            pl.BlockSpec((8, wide_x), lambda i: (last, 0)),
            pl.BlockSpec((8, wide_b), lambda i: (last, 0)),
            pl.BlockSpec((8, wide_b), lambda i: (last, 0)),
        ],
        out_specs=pl.BlockSpec((8, wide_x + 2 * wide_b), lambda i: (0, 0)),
        out_shape=jax.ShapeDtypeStruct((8, wide_x + 2 * wide_b), BF16),
        name="edge",
    )(x, b, c)


def conv_into(raw_ref, tail_ref, weight_ref, lo, pad_ref, out_ref):
    rows, width = raw_ref.shape
    raw = raw_ref[...].astype(F32)
    pad_ref[0:8, lo : lo + width] = tail_ref[:, lo : lo + width]
    pad_ref[8 : 8 + rows, lo : lo + width] = raw
    tail_ref[:, lo : lo + width] = raw[rows - 8 :]
    total = weight_ref[TAPS - 1 : TAPS, :] * raw
    for back in range(1, TAPS):
        tap = TAPS - 1 - back
        total = total + weight_ref[tap : tap + 1, :] * pad_ref[8 - back : 8 - back + rows, lo : lo + width]
    out_ref[...] = silu(total).astype(BF16)


def front_kernel(
    first_ref,
    x_ref,
    b_ref,
    c_ref,
    halo_ref,
    dt_ref,
    alog_ref,
    cx_ref,
    cb_ref,
    cc_ref,
    init_ref,
    xo_ref,
    bo_ref,
    co_ref,
    cum_ref,
    key_ref,
    fresh_ref,
    drop_ref,
    start_ref,
    msg_ref,
    pad_ref,
    tail_ref,
    weight_ref,
    state_ref,
):
    step = pl.program_id(0)
    wide_x, wide_b = x_ref.shape[1], b_ref.shape[1]
    heads, tokens = dt_ref.shape
    subs = tokens // SUB
    groups = wide_b // STATE
    lanes = wide_x // groups

    @pl.when(step == 0)
    def _():
        tail_ref[...] = halo_ref[...].astype(F32)
        raw = dt_ref[...]
        grown = jnp.exp(-jnp.abs(raw))
        near = 1.0 + grown
        gap = near - 1.0
        log_near = jnp.where(gap == 0.0, grown, jnp.log(near) * grown / jnp.where(gap == 0.0, 1.0, gap))
        size = jnp.maximum(raw, 0.0) + log_near
        rate = size * (-LOG2E * jnp.exp(column_of(alog_ref, heads)))
        lane = lax.broadcasted_iota(jnp.int32, (heads, SUB), 1)
        rows = []
        for j in range(subs):
            cum = rate[:, j * SUB : (j + 1) * SUB]
            shift = 1
            while shift < SUB:
                cum = cum + jnp.where(lane >= shift, pltpu.roll(cum, shift, 1), 0.0)
                shift *= 2
            size_j = size[:, j * SUB : (j + 1) * SUB]
            last = cum[:, SUB - 1 : SUB]
            cum_ref[:, j * SUB : (j + 1) * SUB] = cum
            key_ref[:, j * SUB : (j + 1) * SUB] = cum - jnp.log(size_j) * LOG2E
            weight_ref[:, j * SUB : (j + 1) * SUB] = jnp.exp2(last - cum) * size_j
            rows.append(widen_row(jnp.exp2(last), wide_x))
        rows += [jnp.ones((1, wide_x), F32)] * (8 - subs)
        drop_ref[...] = jnp.concatenate(rows, axis=0)

        @pl.when(first_ref[0] == 1)
        def _():
            for k in range(wide_x // STATE):
                state_ref[:, k * STATE : (k + 1) * STATE] = init_ref[k * STATE : (k + 1) * STATE, :].T

        @pl.when(first_ref[0] != 1)
        def _():
            state_ref[...] = jnp.zeros_like(state_ref)

        start_ref[...] = state_ref[...]

    conv_into(x_ref, tail_ref, cx_ref, 0, pad_ref, xo_ref)
    conv_into(b_ref, tail_ref, cb_ref, wide_x, pad_ref, bo_ref)
    conv_into(c_ref, tail_ref, cc_ref, wide_x + wide_b, pad_ref, co_ref)

    per_step = x_ref.shape[0] // SUB
    for k in range(per_step):
        at = pl.multiple_of(step * (per_step * SUB) + k * SUB, SUB)
        spread = widen_tokens(weight_ref[:, pl.ds(at, SUB)], wide_x)
        inner = (spread * xo_ref[k * SUB : (k + 1) * SUB, :].astype(F32)).astype(BF16)
        fall = drop_ref[pl.ds(step * per_step + k, 1), :]
        for g in range(groups):
            fresh = dot(
                bo_ref[k * SUB : (k + 1) * SUB, g * STATE : (g + 1) * STATE],
                inner[:, g * lanes : (g + 1) * lanes],
                ((0,), (0,)),
            )
            fresh_ref[k, :, g * lanes : (g + 1) * lanes] = fresh
            state_ref[:, g * lanes : (g + 1) * lanes] = (
                fall[:, g * lanes : (g + 1) * lanes] * state_ref[:, g * lanes : (g + 1) * lanes] + fresh
            )

    @pl.when(step == pl.num_programs(0) - 1)
    def _():
        tiles = STATE // 8
        whole = drop_ref[0:1, :]
        for j in range(1, subs):
            whole = whole * drop_ref[j : j + 1, :]
        high = whole.astype(BF16).astype(F32)
        low = whole - high
        for g in range(groups):
            own = state_ref[:, g * lanes : (g + 1) * lanes].reshape(tiles, 8, lanes)
            msg_ref[g * tiles : (g + 1) * tiles, :, :lanes] = own.astype(BF16)
            pieces = [
                part[:, g * lanes + q * 128 : g * lanes + (q + 1) * 128]
                for part in (high, low)
                for q in range(lanes // 128)
            ]
            tile = jnp.concatenate(pieces, axis=0)
            msg_ref[g * tiles : (g + 1) * tiles, :, lanes:] = jnp.broadcast_to(
                tile[None], (tiles, 8, 128)
            ).astype(BF16)


def front(first, x, b, c, halo, dt, a_log, conv_x, conv_b, conv_c, init):
    tokens, wide_x = x.shape
    wide_b = b.shape[1]
    heads = dt.shape[0]
    subs = tokens // SUB
    groups = wide_b // STATE
    lanes = wide_x // groups
    parts = groups * STATE // 8
    per_step = CHUNK // SUB

    def whole(*shape):
        return pl.BlockSpec(shape, lambda i, *_: (0,) * len(shape))

    return pl.pallas_call(
        front_kernel,
        grid_spec=pltpu.PrefetchScalarGridSpec(
            num_scalar_prefetch=1,
            grid=(tokens // CHUNK,),
            in_specs=[
                pl.BlockSpec((CHUNK, wide_x), lambda i, *_: (i, 0)),
                pl.BlockSpec((CHUNK, wide_b), lambda i, *_: (i, 0)),
                pl.BlockSpec((CHUNK, wide_b), lambda i, *_: (i, 0)),
                whole(8, wide_x + 2 * wide_b),
                whole(heads, tokens),
                pl.BlockSpec(memory_space=pltpu.SMEM),
                whole(TAPS, wide_x),
                whole(TAPS, wide_b),
                whole(TAPS, wide_b),
                whole(wide_x, STATE),
            ],
            out_specs=[
                pl.BlockSpec((CHUNK, wide_x), lambda i, *_: (i, 0)),
                pl.BlockSpec((CHUNK, wide_b), lambda i, *_: (i, 0)),
                pl.BlockSpec((CHUNK, wide_b), lambda i, *_: (i, 0)),
                whole(heads, tokens),
                whole(heads, tokens),
                pl.BlockSpec((per_step, STATE, wide_x), lambda i, *_: (i, 0, 0)),
                whole(8, wide_x),
                whole(STATE, wide_x),
                whole(parts, 8, lanes + 128),
            ],
            scratch_shapes=[
                pltpu.VMEM((CHUNK + 8, wide_x + 2 * wide_b), F32),
                pltpu.VMEM((8, wide_x + 2 * wide_b), F32),
                pltpu.VMEM((heads, tokens), F32),
                pltpu.VMEM((STATE, wide_x), F32),
            ],
        ),
        out_shape=[
            jax.ShapeDtypeStruct((tokens, wide_x), BF16),
            jax.ShapeDtypeStruct((tokens, wide_b), BF16),
            jax.ShapeDtypeStruct((tokens, wide_b), BF16),
            jax.ShapeDtypeStruct((heads, tokens), F32),
            jax.ShapeDtypeStruct((heads, tokens), F32),
            jax.ShapeDtypeStruct((subs, STATE, wide_x), F32),
            jax.ShapeDtypeStruct((8, wide_x), F32),
            jax.ShapeDtypeStruct((STATE, wide_x), F32),
            jax.ShapeDtypeStruct((parts, 8, lanes + 128), BF16),
        ],
        name="front",
    )(first, x, b, c, halo, dt, a_log, conv_x, conv_b, conv_c, init)


def scan_kernel(msg_ref, out_ref):
    slabs, _, wide = msg_ref.shape
    lanes = wide - 128
    pieces = lanes // 128
    running = [jnp.zeros((8, 128), F32) for _ in range(pieces)]
    for s in range(slabs):
        falls = msg_ref[s, :, lanes:].astype(F32)
        for q in range(pieces):
            out_ref[s, :, q * 128 : (q + 1) * 128] = running[q].astype(BF16)
            fall = falls[q : q + 1, :] + falls[pieces + q : pieces + q + 1, :]
            running[q] = fall * running[q] + msg_ref[s, :, q * 128 : (q + 1) * 128].astype(F32)


def scan_slabs(msg):
    slabs, _, wide = msg.shape
    return pl.pallas_call(
        scan_kernel,
        out_shape=jax.ShapeDtypeStruct((slabs, 8, wide - 128), BF16),
        name="scan",
    )(msg)


def chunk_kernel(
    x_ref,
    b_ref,
    c_ref,
    z_ref,
    cum_ref,
    key_ref,
    fresh_ref,
    drop_ref,
    skip_ref,
    gain_ref,
    came_ref,
    start_ref,
    top_ref,
    bottom_ref,
    next_ref,
    state_ref,
    *,
    base,
):
    step = pl.program_id(0)
    wide_x, wide_b = x_ref.shape[1], b_ref.shape[1]
    groups = wide_b // STATE
    lanes = wide_x // groups
    heads = cum_ref.shape[0]
    per_group = heads // groups

    @pl.when(step == 0)
    def _():
        if base == 0:
            tiles = STATE // 8
            for g in range(groups):
                came = came_ref[g * tiles : (g + 1) * tiles].astype(F32).reshape(STATE, lanes)
                state_ref[:, g * lanes : (g + 1) * lanes] = (
                    came + start_ref[:, g * lanes : (g + 1) * lanes]
                )
        else:
            state_ref[...] = came_ref[...]

    cum = cum_ref[...]
    cum_cols = cum.T
    spread = widen_tokens(jnp.exp2(cum), wide_x)
    fall = drop_ref[pl.ds(base + step, 1), :]
    row = lax.broadcasted_iota(jnp.int32, (SUB, SUB), 0)
    col = lax.broadcasted_iota(jnp.int32, (SUB, SUB), 1)
    causal = row >= col
    low_half = col < HEAD_SIZE
    for g in range(groups):
        sl = slice(g * lanes, (g + 1) * lanes)
        b_g = b_ref[:, g * STATE : (g + 1) * STATE]
        c_g = c_ref[:, g * STATE : (g + 1) * STATE]
        scores = jnp.where(causal, dot(c_g, b_g, ((1,), (1,))), 0.0)
        pieces = []
        for q in range(per_group // 2):
            mixes = []
            for h in (g * per_group + 2 * q, g * per_group + 2 * q + 1):
                gap = jnp.minimum(cum_cols[:, h : h + 1] - key_ref[h : h + 1, :], 100.0)
                mixes.append((scores * jnp.exp2(gap)).astype(BF16))
            pair = x_ref[:, g * lanes + q * 128 : g * lanes + (q + 1) * 128]
            none = jnp.zeros_like(pair)
            both = jnp.concatenate(
                [jnp.where(low_half, pair, none), jnp.where(low_half, none, pair)], axis=0
            )
            pieces.append(dot(jnp.concatenate(mixes, axis=1), both))
        state = state_ref[:, sl]
        out = jnp.concatenate(pieces, axis=1) + dot(c_g, state.astype(BF16)) * spread[:, sl]
        skip = jnp.concatenate(
            [
                jnp.where(low_half[:1], skip_ref[h], skip_ref[h + 1])
                for h in range(g * per_group, (g + 1) * per_group, 2)
            ],
            axis=1,
        )
        out = out + skip * x_ref[:, sl].astype(F32)
        gated = out * silu(z_ref[:, sl].astype(F32))
        mean_sq = jnp.sum(gated * gated, axis=1, keepdims=True) * (1.0 / lanes)
        normed = (gated * lax.rsqrt(mean_sq + EPSILON) * gain_ref[:, sl]).astype(BF16)

        @pl.when(step == 0)
        def _():
            top_ref[:, sl] = normed

        @pl.when(step == 1)
        def _():
            bottom_ref[:, sl] = normed

        state_ref[:, sl] = fall[:, sl] * state + fresh_ref[0, :, sl]

    next_ref[...] = state_ref[...]


def chunk_out(index, x, b, c, z, cum, key, fresh, drop, skip, gain, came, start):
    wide_x, wide_b = x.shape[1], b.shape[1]
    heads = cum.shape[0]
    base = index * (CHUNK // SUB)

    def whole(shape):
        return pl.BlockSpec(shape, lambda i: (0,) * len(shape))

    def body(*refs):
        chunk_kernel(*refs, base=base)

    return pl.pallas_call(
        body,
        grid=(CHUNK // SUB,),
        in_specs=[
            pl.BlockSpec((SUB, wide_x), lambda i: (base + i, 0)),
            pl.BlockSpec((SUB, wide_b), lambda i: (base + i, 0)),
            pl.BlockSpec((SUB, wide_b), lambda i: (base + i, 0)),
            pl.BlockSpec((SUB, wide_x), lambda i: (base + i, 0)),
            pl.BlockSpec((heads, SUB), lambda i: (0, base + i)),
            pl.BlockSpec((heads, SUB), lambda i: (0, base + i)),
            pl.BlockSpec((1, STATE, wide_x), lambda i: (base + i, 0, 0)),
            whole(drop.shape),
            pl.BlockSpec(memory_space=pltpu.SMEM),
            whole(gain.shape),
            whole(came.shape),
            whole(start.shape),
        ],
        out_specs=[whole((SUB, wide_x)), whole((SUB, wide_x)), whole((STATE, wide_x))],
        out_shape=[
            jax.ShapeDtypeStruct((SUB, wide_x), BF16),
            jax.ShapeDtypeStruct((SUB, wide_x), BF16),
            jax.ShapeDtypeStruct((STATE, wide_x), F32),
        ],
        scratch_shapes=[pltpu.VMEM((STATE, wide_x), F32)],
        name="chunk",
    )(x, b, c, z, cum, key, fresh, drop, skip, gain, came, start)


def weight_spec(cols, which):
    return pl.BlockSpec(
        (None, 16, None, 64, cols),
        lambda n, at, which=which: (at[2 * which], 0, at[2 * which + 1], 0, n),
    )


def stacked(refs):
    return jnp.concatenate([ref[...] for ref in refs], axis=0)


def rows_of(ref):
    return ref[...].reshape(ref.shape[0] * ref.shape[1], ref.shape[2])


def near_kernel(at_ref, *refs, kinds):
    per = (len(refs) - 1 - kinds) // kinds
    out_ref = refs[-1]
    total = None
    for n in range(kinds):
        term = dot(stacked(refs[n * per : (n + 1) * per]), rows_of(refs[kinds * per + n]))
        total = term if total is None else total + term
    out_ref[...] = total


def project_near(at, pieces, weight, cols=256):
    kinds = len(pieces)
    flat = [p for kind in pieces for p in kind]
    rows = sum(p.shape[0] for p in pieces[0])
    width = weight.shape[-1]

    def body(*refs):
        near_kernel(*refs, kinds=kinds)

    return pl.pallas_call(
        body,
        grid_spec=pltpu.PrefetchScalarGridSpec(
            num_scalar_prefetch=1,
            grid=(width // cols,),
            in_specs=[pl.BlockSpec(p.shape, lambda n, *_: (0, 0)) for p in flat]
            + [weight_spec(cols, n) for n in range(kinds)],
            out_specs=pl.BlockSpec((rows, cols), lambda n, *_: (0, n)),
        ),
        out_shape=jax.ShapeDtypeStruct((rows, width), F32),
        name="near",
    )(at, *flat, *([weight] * kinds))


def far_kernel(at_ref, *refs, count):
    rows = stacked(refs[:count])
    w_ref, acc_ref, out_ref = refs[count], refs[count + 1], refs[-1]
    out_ref[...] = (acc_ref[...] + dot(rows, rows_of(w_ref))).astype(BF16)


def project_far(at, pieces, weight, acc, block, before=None, cols=512):
    rows = sum(p.shape[0] for p in pieces)
    total, width = acc.shape
    extra = [] if before is None else [before]

    def body(*refs):
        far_kernel(*refs, count=len(pieces))

    return pl.pallas_call(
        body,
        grid_spec=pltpu.PrefetchScalarGridSpec(
            num_scalar_prefetch=1,
            grid=(width // cols,),
            in_specs=[pl.BlockSpec(p.shape, lambda n, *_: (0, 0)) for p in pieces]
            + [weight_spec(cols, 0), pl.BlockSpec((rows, cols), lambda n, *_: (block, n))]
            + [pl.BlockSpec(memory_space=pl.ANY)] * len(extra),
            out_specs=pl.BlockSpec((rows, cols), lambda n, *_: (block, n)),
        ),
        out_shape=jax.ShapeDtypeStruct((total, width), BF16),
        input_output_aliases={} if before is None else {len(pieces) + 3: 0},
        name="far",
    )(at, *pieces, weight, acc, *extra)


def turn(value, axis, distance):
    count = lax.axis_size(axis)
    return lax.ppermute(value, axis, [(i, (i + distance) % count) for i in range(count)])


def local(
    x_in,
    b_in,
    c_in,
    z_in,
    dt_in,
    a_log,
    skip_gain,
    norm_gain,
    conv_x,
    conv_b,
    conv_c,
    init_state,
    out_weight,
):
    tokens, wide_x = x_in.shape[1:]
    slabs = lax.axis_size("seq")
    head, part = lax.axis_index("head"), lax.axis_index("dp")
    x, b, c, z, dt = x_in[0], b_in[0], c_in[0], z_in[0], dt_in[0]
    halo = lax.ppermute(edge_rows(x, b, c), "seq", [(i, i + 1) for i in range(slabs - 1)])
    other_rows = turn(out_weight, "dp", 1)
    first = (lax.axis_index("seq") == 0).astype(jnp.int32).reshape(1)
    x, b, c, cum, key, fresh, drop, start, msg = front(
        first, x, b, c, halo, dt, a_log, conv_x, conv_b, conv_c, init_state.reshape(wide_x, STATE)
    )
    msg, other_rows = lax.optimization_barrier((msg, other_rows))
    weight = lax.all_gather(jnp.stack([out_weight, other_rows]), "seq", axis=0)
    weight = weight.reshape(2, slabs // 2, 2, *out_weight.shape)
    msg = lax.all_to_all(msg, "seq", 0, 0, tiled=True)
    came = lax.all_to_all(scan_slabs(msg), "seq", 0, 0, tiled=True)

    gain = norm_gain.reshape(1, wide_x)
    count = tokens // CHUNK
    own, ahead, behind, beyond = [], [], [], []
    for index in range(count):
        top, bottom, came = chunk_out(
            index, x, b, c, z, cum, key, fresh, drop, skip_gain, gain, came, start
        )
        own += [top, bottom]
        top_back, bottom_ahead = turn(top, "head", 1), turn(bottom, "head", -1)
        bottom_back, top_ahead = turn(bottom, "head", 1), turn(top, "head", -1)
        behind += [top_back, bottom_back]
        ahead += [top_ahead, bottom_ahead]
        beyond += [turn(top_back, "head", 1), turn(bottom_ahead, "head", -1)]

    def place(owner):
        return [owner % 2, (owner // 2 + part) % 2]

    table = [place((head + step) % 4) for step in (0, 1, 3)]
    near_at = jnp.stack([v for pair in table for v in pair]).astype(jnp.int32)
    far_at = jnp.stack(place((head + 2) % 4)).astype(jnp.int32)
    acc = project_near(near_at, (own, ahead, behind), weight)
    split = 2 * (count - 1)
    out = project_far(far_at, beyond[:split], weight, acc, 0)
    out = project_far(far_at, beyond[split:], weight, acc, count - 1, before=out)
    return out[None]


def solution(mesh):
    in_specs = (
        P("dp", "seq", "head"),
        P("dp", "seq", "head"),
        P("dp", "seq", "head"),
        P("dp", "seq", "head"),
        P("dp", "head", "seq"),
        P("head"),
        P("head"),
        P("head"),
        P(None, "head"),
        P(None, "head"),
        P(None, "head"),
        P("dp", "head", None, None),
        P(("dp", "seq"), "head"),
    )
    out_specs = P("dp", "seq", "head")

    return jax.shard_map(local, mesh=mesh, in_specs=in_specs, out_specs=out_specs, check_vma=False)
```

time: 394 us -> 209 us (0.53)
  the two profiles are of different devices: /device:TPU:65 before, /device:TPU:2 now
where the time goes in v1:
time: 209 us; the launch traced here: 208 us
  starting transfers between devices  63.1 us (30%)
  Pallas kernels  58.9 us (28%)
  waiting for transfers between devices  35.9 us (17%)
  blocking collectives  31.3 us (15%)
  between operations  13.6 us (7%)
  local copies, waits for them, and re-layouts  3.45 us (2%)
    ppermute x19, starting transfers between devices, turn(): lax.ppermute(value, axis, [(i, (i + distance) % count) for i in range(cou...  61.2 us
    ppermute x19, waiting for transfers between devices, turn(): lax.ppermute(value, axis, [(i, (i + distance) % count) for i in range(cou...  32.4 us
    pallas_call x1, Pallas kernels, project_near(): pl.pallas_call(body, grid_spec=pltpu.PrefetchScalarGridSpec(num_scalar_pr...  16.7 us
    pallas_call x3, Pallas kernels, chunk_out(): pl.pallas_call(body, grid=(CHUNK // SUB,), in_specs=[pl.BlockSpec((SUB, w...  16.7 us
    all_to_all x1, blocking collectives, local(): msg = lax.all_to_all(msg, 'seq', 0, 0, tiled=True)  16 us
    all_to_all x1, blocking collectives, local(): came = lax.all_to_all(scan_slabs(msg), 'seq', 0, 0, tiled=True)  15.3 us
    pallas_call x2, Pallas kernels, project_far(): pl.pallas_call(body, grid_spec=pltpu.PrefetchScalarGridSpec(num_scalar_pr...  13.4 us
    pallas_call x1, Pallas kernels, front(): pl.pallas_call(front_kernel, grid_spec=pltpu.PrefetchScalarGridSpec(num_s...  8.99 us
  transfers between devices with their start and end apart: 21, of which 9 were waited for; matrix products, arithmetic and copies ran while one was open for 1% of the time, Pallas kernels for 25%

profile of v1, /device:TPU:2, one launch (start us, length us, event | category | flops | bytes accessed | tf_op | source)
XLA Modules:
  0.0 207.7 jit_solution(8059766245941880287)
XLA Ops:
  6.5 1.9 collective-permute-start.1
  8.5 1.3 edge.1
  9.8 1.9 collective-permute-start
  11.7 3.4 %collective-permute-done.halo_ref = bf16[8,1536]{1,0:T(8,128)(2,1)S(1)} collective-permute-done((bf16[8,1536]{1,0:T(8,128)(2,1)}, bf16[8,1536]{1,0:T(8,128)(2,1)S(1)}, u32[]{:S(2)}, u32[]{:S(2)}) %collective-permute-start) | collective-permute-done | bytes 24608 | tf_op jit(solution)/shard_map/ppermute | solution.py:533
  15.1 0.6 copy-done.18
  15.8 9.0 %front.1 = (bf16[768,1024]{1,0:T(8,128)(2,1)}, bf16[768,256]{1,0:T(8,128)(2,1)}, bf16[768,256]{1,0:T(8,128)(2,1)}, f32[16,768]{1,0:T(8,128)}, f32[16,768]{1,0:T(...) custom-call(s32[1]{0:T(128)} %bitcast.2.first_ref, ...), custom_call_target="tpu_custom_call" | custom-call | tf_op jit(solution)/shard_map/front/pallas_call | solution.py:229
  24.8 0.8 pad_maximum_fusion
  25.6 0.0 all-gather.3.cloned.1.call-update
  25.6 16.0 %all_to_all.10.msg_ref = bf16[32,8,640]{2,1,0:T(8,128)(2,1)} all-to-all(bf16[32,8,640]{2,1,0:T(8,128)(2,1)} %get-tuple-element.32), channel_id=1, replica_groups=mesh['dp'=2,'seq'=32,'head'=4] {'seq'}, dimensions={0} | all-to-all | bytes 655360 | tf_op jit(solution)/shard_map/all_to_all | solution.py:542
  41.6 1.8 scan.1
  43.4 15.3 %all_to_all.11.refs_10_ = bf16[32,8,512]{2,1,0:T(8,128)(2,1)} all-to-all(bf16[32,8,512]{2,1,0:T(8,128)(2,1)} %scan.1), channel_id=1, replica_groups=mesh['dp'=2,'seq'=32,'head'=4] {'seq'}, dimensions={0} | all-to-all | bytes 524288 | tf_op jit(solution)/shard_map/all_to_all | solution.py:543
  58.7 5.5 %chunk.3 = (bf16[128,1024]{1,0:T(8,128)(2,1)}, bf16[128,1024]{1,0:T(8,128)(2,1)}, f32[128,1024]{1,0:T(8,128)}) custom-call(bf16[768,1024]{1,0:T(8,128)(2,1)} %get-tuple-element.24.refs_0_, bf16[768,256]{1,0:T(8,128)(2,1)} %get-tuple-element.25.refs_1_, bf16[768,256]{1,0:T(8,128)(2,1)} %get-tuple-element.26.refs_2_, bf16[768,1024]{1,0:T(8,128)(2,1)} %bitcast.25, ...), custom_call_target="tpu_custom_call" | custom-call | tf_op jit(solution)/shard_map/chunk/pallas_call | solution.py:403
  64.2 2.8 %collective-permute-start.11 = (bf16[128,1024]{1,0:T(8,128)(2,1)}, bf16[128,1024]{1,0:T(8,128)(2,1)S(1)}, u32[]{:S(2)}, u32[]{:S(2)}) collective-permute-start(bf16[128,1024]{1,0:T(8,128)(2,1)} %get-tuple-element.39.refs_1_), channel_id=1, source_target_pairs={{0,1},{1,2},{2,3},{3,0},{4,5},{5,6},{6,7},{7,4},{8,9},{9,10},{10,1... | collective-permute-start | bytes 786440 | tf_op jit(solution)/shard_map/ppermute | solution.py:511
  67.0 1.7 collective-permute-start.6
  68.7 2.1 %collective-permute-start.12 = (bf16[128,1024]{1,0:T(8,128)(2,1)}, bf16[128,1024]{1,0:T(8,128)(2,1)S(1)}, u32[]{:S(2)}, u32[]{:S(2)}) collective-permute-start(bf16[128,1024]{1,0:T(8,128)(2,1)} %get-tuple-element.40.refs_2_), channel_id=1, source_target_pairs={{0,1},{1,2},{2,3},{3,0},{4,5},{5,6},{6,7},{7,4},{8,9},{9,10},{10,1... | collective-permute-start | bytes 786440 | tf_op jit(solution)/shard_map/ppermute | solution.py:511
  70.8 2.0 collective-permute-start.7
  72.8 5.5 %chunk.4 = (bf16[128,1024]{1,0:T(8,128)(2,1)}, bf16[128,1024]{1,0:T(8,128)(2,1)}, f32[128,1024]{1,0:T(8,128)}) custom-call(bf16[768,1024]{1,0:T(8,128)(2,1)} %get-tuple-element.24.refs_0_, bf16[768,256]{1,0:T(8,128)(2,1)} %get-tuple-element.25.refs_1_, bf16[768,256]{1,0:T(8,128)(2,1)} %get-tuple-element.26.refs_2_, bf16[768,1024]{1,0:T(8,128)(2,1)} %bitcast.26, ...), custom_call_target="tpu_custom_call" | custom-call | tf_op jit(solution)/shard_map/chunk/pallas_call | solution.py:403
  78.3 5.7 %chunk.5 = (bf16[128,1024]{1,0:T(8,128)(2,1)}, bf16[128,1024]{1,0:T(8,128)(2,1)}, f32[128,1024]{1,0:T(8,128)}) custom-call(bf16[768,1024]{1,0:T(8,128)(2,1)} %get-tuple-element.24.refs_0_, bf16[768,256]{1,0:T(8,128)(2,1)} %get-tuple-element.25.refs_1_, bf16[768,256]{1,0:T(8,128)(2,1)} %get-tuple-element.26.refs_2_, bf16[768,1024]{1,0:T(8,128)(2,1)} %bitcast.27, ...), custom_call_target="tpu_custom_call" | custom-call | tf_op jit(solution)/shard_map/chunk/pallas_call | solution.py:403
  84.0 2.1 collective-permute-start.10
  86.1 0.9 collective-permute-start.2
  87.0 2.1 collective-permute-done.6.refs_7_
  89.0 3.6 %collective-permute-start.15 = (bf16[128,1024]{1,0:T(8,128)(2,1)}, bf16[128,1024]{1,0:T(8,128)(2,1)S(1)}, u32[]{:S(2)}, u32[]{:S(2)}) collective-permute-start(bf16[128,1024]{1,0:T(8,128)(2,1)} %get-tuple-element.37.refs_6_), channel_id=1, source_target_pairs={{0,1},{1,2},{2,3},{3,0},{4,5},{5,6},{6,7},{7,4},{8,9},{9,10},{10,1... | collective-permute-start | bytes 786440 | tf_op jit(solution)/shard_map/ppermute | solution.py:511
  92.7 0.5 collective-permute-start.4
  93.2 1.5 collective-permute-done.7.refs_8_
  94.7 15.7 %collective-permute-start.13 = (bf16[128,1024]{1,0:T(8,128)(2,1)S(1)}, bf16[128,1024]{1,0:T(8,128)(2,1)S(1)}, u32[]{:S(2)}, u32[]{:S(2)}) collective-permute-start(bf16[128,1024]{1,0:T(8,128)(2,1)S(1)} %copy-done.4), channel_id=1, source_target_pairs={{0,1},{1,2},{2,3},{3,0},{4,5},{5,6},{6,7},{7,4},{8,9},{9,10},{10,1... | collective-permute-start | bytes 786440 | tf_op jit(solution)/shard_map/ppermute | solution.py:511
  110.4 4.7 %collective-permute-start.8 = (bf16[128,1024]{1,0:T(8,128)(2,1)S(1)}, bf16[128,1024]{1,0:T(8,128)(2,1)S(1)}, u32[]{:S(2)}, u32[]{:S(2)}) collective-permute-start(bf16[128,1024]{1,0:T(8,128)(2,1)S(1)} %copy-done.4), channel_id=1, source_target_pairs={{0,3},{1,0},{2,1},{3,2},{4,7},{5,4},{6,5},{7,6},{8,11},{9,8},{10,9... | collective-permute-start | bytes 786440 | tf_op jit(solution)/shard_map/ppermute | solution.py:511
  115.1 1.7 collective-permute-done.2.refs_17_
  116.8 12.2 %collective-permute-start.9 = (bf16[128,1024]{1,0:T(8,128)(2,1)S(1)}, bf16[128,1024]{1,0:T(8,128)(2,1)S(1)}, u32[]{:S(2)}, u32[]{:S(2)}) collective-permute-start(bf16[128,1024]{1,0:T(8,128)(2,1)S(1)} %copy-done.5), channel_id=1, source_target_pairs={{0,3},{1,0},{2,1},{3,2},{4,7},{5,4},{6,5},{7,6},{8,11},{9,8},{10,9... | collective-permute-start | bytes 786440 | tf_op jit(solution)/shard_map/ppermute | solution.py:511
  129.1 0.7 collective-permute-start.14
  129.8 5.6 %collective-permute-done.4.refs_12_ = bf16[128,1024]{1,0:T(8,128)(2,1)S(1)} collective-permute-done((bf16[128,1024]{1,0:T(8,128)(2,1)}, bf16[128,1024]{1,0:T(8,128)(2,1)S(1)}, u32[]{:S(2)}, u32[]{:S(2)}) %collective-permute-start.4) | collective-permute-done | bytes 262176 | tf_op jit(solution)/shard_map/ppermute | solution.py:511
  135.4 1.3 collective-permute-start.16
  136.7 2.9 %collective-permute-start.17 = (bf16[128,1024]{1,0:T(8,128)(2,1)S(1)}, bf16[128,1024]{1,0:T(8,128)(2,1)}, u32[]{:S(2)}, u32[]{:S(2)}) collective-permute-start(bf16[128,1024]{1,0:T(8,128)(2,1)S(1)} %collective-permute-done.7.refs_8_), channel_id=1, source_target_pairs={{0,3},{1,0},{2,1},{3,2},{4,7},{5,4},{6,5},{7,6},{8,11},{9,8},{10,9... | collective-permute-start | bytes 786440 | tf_op jit(solution)/shard_map/ppermute | solution.py:511
  139.5 4.4 %collective-permute-done.8.refs_9_ = bf16[128,1024]{1,0:T(8,128)(2,1)S(1)} collective-permute-done((bf16[128,1024]{1,0:T(8,128)(2,1)S(1)}, bf16[128,1024]{1,0:T(8,128)(2,1)S(1)}, u32[]{:S(2)}, u32[]{:S(2)}) %collective-permute-start.8) | collective-permute-done | bytes 262176 | tf_op jit(solution)/shard_map/ppermute | solution.py:511
  143.9 1.3 collective-permute-start.18
  145.3 5.8 %collective-permute-done.9.refs_10_ = bf16[128,1024]{1,0:T(8,128)(2,1)S(1)} collective-permute-done((bf16[128,1024]{1,0:T(8,128)(2,1)S(1)}, bf16[128,1024]{1,0:T(8,128)(2,1)S(1)}, u32[]{:S(2)}, u32[]{:S(2)}) %collective-permute-start.9) | collective-permute-done | bytes 262176 | tf_op jit(solution)/shard_map/ppermute | solution.py:511
  151.1 2.1 collective-permute-start.19
  153.1 6.8 %collective-permute-done.14.refs_16_ = bf16[128,1024]{1,0:T(8,128)(2,1)S(1)} collective-permute-done((bf16[128,1024]{1,0:T(8,128)(2,1)S(1)}, bf16[128,1024]{1,0:T(8,128)(2,1)S(1)}, u32[]{:S(2)}, u32[]{:S(2)}) %collective-permute-start.14) | collective-permute-done | bytes 262176 | tf_op jit(solution)/shard_map/ppermute | solution.py:511
  159.9 1.1 collective-permute-start.3
  161.1 4.5 %collective-permute-done.16.refs_1_ = bf16[128,1024]{1,0:T(8,128)(2,1)S(1)} collective-permute-done((bf16[128,1024]{1,0:T(8,128)(2,1)S(1)}, bf16[128,1024]{1,0:T(8,128)(2,1)S(1)}, u32[]{:S(2)}, u32[]{:S(2)}) %collective-permute-start.16) | collective-permute-done | bytes 262176 | tf_op jit(solution)/shard_map/ppermute | solution.py:511
  165.6 0.7 copy-done.13
  166.3 1.6 collective-permute-start.5
  167.9 0.7 stack.51.refs_0_
  168.6 0.6 pad_add_fusion.refs_0_
  169.3 16.7 %near.1.refs_6_.refs_4_ = f32[768,2048]{1,0:T(8,128)} custom-call(s32[6]{0:T(128)} %stack.51.refs_0_, bf16[128,1024]{1,0:T(8,128)(2,1)} %get-tuple-element.39.refs_1_, bf16[128,1024]{1,0:T(8,128)(2,1)} %get-tuple-element.40.refs_2_, bf16[128,1024]{1,0:T(8,128)(2,1)} %get-tuple-element.41.refs_3_, bf16[128,1024]{1,0:T(8,128)(2,1)} %get-tuple-element.42.refs_4_, ...), custom_call_target="tpu_custom_call" | custom-call | tf_op jit(solution)/shard_map/near/pallas_call | solution.py:465
  186.1 0.7 copy-done.15
  186.7 7.4 %far.2.refs_5_ = bf16[768,2048]{1,0:T(8,128)(2,1)} custom-call(s32[2]{0:T(128)} %pad_add_fusion.refs_0_, bf16[128,1024]{1,0:T(8,128)(2,1)} %copy-done.13, bf16[128,1024]{1,0:T(8,128)(2,1)} %collective-permute-done.17.refs_2_, bf16[128,1024]{1,0:T(8,128)(2,1)} %copy-done.15, bf16[128,1024]{1,0:T(8,128)(2,1)} %collective-permute-done.19.refs_4_, ...), custom_call_target="tpu_custom_call" | custom-call | tf_op jit(solution)/shard_map/far/pallas_call | solution.py:493
  194.2 0.7 copy-done.16
  194.9 6.0 %far.3 = bf16[768,2048]{1,0:T(8,128)(2,1)} custom-call(s32[2]{0:T(128)} %pad_add_fusion.refs_0_, bf16[128,1024]{1,0:T(8,128)(2,1)} %copy-done.16, bf16[128,1024]{1,0:T(8,128)(2,1)} %collective-permute-done.5.refs_2_, bf16[2,16,2,64,2048]{4,3,2,1,0:T(8,128)(2,1)} %bitcast.24, f32[768,2048]{1,0:T(8,128)} %near.1.refs_6_.refs_4_, ...), custom_call_target="tpu_custom_call", output_to_operand_aliasing={{}: (5, {})} | custom-call | tf_op jit(solution)/shard_map/far/pallas_call | solution.py:493
  (47 shorter events, 0.1 us)
Async XLA Ops:
  6.5 18.2 %copy-start.17 = (bf16[64,2048]{1,0:T(8,128)(2,1)S(1)}, bf16[64,2048]{1,0:T(8,128)(2,1)}, u32[]{:S(2)}) copy-start(bf16[64,2048]{1,0:T(8,128)(2,1)} %param.25) | copy-start | bytes 786436
  6.5 162.7 %all-gather.3.cloned.1.call-start = ((), (), s32[]{:S(2)}) async-start(), calls=%async_computation.2 | async-start | bytes 17301504 | tf_op jit(solution)/shard_map/all_gather | solution.py:540
  6.5 18.2 %collective-permute-start.1 = (bf16[64,2048]{1,0:T(8,128)(2,1)}, bf16[64,2048]{1,0:T(8,128)(2,1)S(1)}, u32[]{:S(2)}, u32[]{:S(2)}) collective-permute-start(bf16[64,2048]{1,0:T(8,128)(2,1)} %param.25), channel_id=1, source_target_pairs={{0,128},{128,0},{1,129},{129,1},{2,130},{130,2},{3,131},{131,3},{4... | collective-permute-start | bytes 786440 | tf_op jit(solution)/shard_map/ppermute | solution.py:511
  9.8 5.3 %collective-permute-start = (bf16[8,1536]{1,0:T(8,128)(2,1)}, bf16[8,1536]{1,0:T(8,128)(2,1)S(1)}, u32[]{:S(2)}, u32[]{:S(2)}) collective-permute-start(bf16[8,1536]{1,0:T(8,128)(2,1)} %edge.1), channel_id=1, source_target_pairs={{0,4},{4,8},{8,12},{12,16},{16,20},{20,24},{24,28},{28,32},{32,36}... | collective-permute-start | bytes 73736 | tf_op jit(solution)/shard_map/ppermute | solution.py:533
  15.1 0.6 copy-start.18
  64.2 21.9 %collective-permute-start.11 = (bf16[128,1024]{1,0:T(8,128)(2,1)}, bf16[128,1024]{1,0:T(8,128)(2,1)S(1)}, u32[]{:S(2)}, u32[]{:S(2)}) collective-permute-start(bf16[128,1024]{1,0:T(8,128)(2,1)} %get-tuple-element.39.refs_1_), channel_id=1, source_target_pairs={{0,1},{1,2},{2,3},{3,0},{4,5},{5,6},{6,7},{7,4},{8,9},{9,10},{10,1... | collective-permute-start | bytes 786440 | tf_op jit(solution)/shard_map/ppermute | solution.py:511
  67.0 22.1 %collective-permute-start.6 = (bf16[128,1024]{1,0:T(8,128)(2,1)}, bf16[128,1024]{1,0:T(8,128)(2,1)S(1)}, u32[]{:S(2)}, u32[]{:S(2)}) collective-permute-start(bf16[128,1024]{1,0:T(8,128)(2,1)} %get-tuple-element.39.refs_1_), channel_id=1, source_target_pairs={{0,3},{1,0},{2,1},{3,2},{4,7},{5,4},{6,5},{7,6},{8,11},{9,8},{10,9... | collective-permute-start | bytes 786440 | tf_op jit(solution)/shard_map/ppermute | solution.py:511
  68.7 24.0 %collective-permute-start.12 = (bf16[128,1024]{1,0:T(8,128)(2,1)}, bf16[128,1024]{1,0:T(8,128)(2,1)S(1)}, u32[]{:S(2)}, u32[]{:S(2)}) collective-permute-start(bf16[128,1024]{1,0:T(8,128)(2,1)} %get-tuple-element.40.refs_2_), channel_id=1, source_target_pairs={{0,1},{1,2},{2,3},{3,0},{4,5},{5,6},{6,7},{7,4},{8,9},{9,10},{10,1... | collective-permute-start | bytes 786440 | tf_op jit(solution)/shard_map/ppermute | solution.py:511
  70.8 23.9 %collective-permute-start.7 = (bf16[128,1024]{1,0:T(8,128)(2,1)}, bf16[128,1024]{1,0:T(8,128)(2,1)S(1)}, u32[]{:S(2)}, u32[]{:S(2)}) collective-permute-start(bf16[128,1024]{1,0:T(8,128)(2,1)} %get-tuple-element.40.refs_2_), channel_id=1, source_target_pairs={{0,3},{1,0},{2,1},{3,2},{4,7},{5,4},{6,5},{7,6},{8,11},{9,8},{10,9... | collective-permute-start | bytes 786440 | tf_op jit(solution)/shard_map/ppermute | solution.py:511
  78.3 16.3 %copy-start.4 = (bf16[128,1024]{1,0:T(8,128)(2,1)S(1)}, bf16[128,1024]{1,0:T(8,128)(2,1)}, u32[]{:S(2)}) copy-start(bf16[128,1024]{1,0:T(8,128)(2,1)} %get-tuple-element.41.refs_3_) | copy-start | bytes 786436
  78.3 38.5 %copy-start.5 = (bf16[128,1024]{1,0:T(8,128)(2,1)S(1)}, bf16[128,1024]{1,0:T(8,128)(2,1)}, u32[]{:S(2)}) copy-start(bf16[128,1024]{1,0:T(8,128)(2,1)} %get-tuple-element.42.refs_4_) | copy-start | bytes 786436
  84.0 26.4 %collective-permute-start.10 = (bf16[128,1024]{1,0:T(8,128)(2,1)}, bf16[128,1024]{1,0:T(8,128)(2,1)S(1)}, u32[]{:S(2)}, u32[]{:S(2)}) collective-permute-start(bf16[128,1024]{1,0:T(8,128)(2,1)} %get-tuple-element.36.refs_5_), channel_id=1, source_target_pairs={{0,3},{1,0},{2,1},{3,2},{4,7},{5,4},{6,5},{7,6},{8,11},{9,8},{10,9... | collective-permute-start | bytes 786440 | tf_op jit(solution)/shard_map/ppermute | solution.py:511
  86.1 83.1 %copy-start = (bf16[128,1024]{1,0:T(8,128)(2,1)}, bf16[128,1024]{1,0:T(8,128)(2,1)S(1)}, u32[]{:S(2)}) copy-start(bf16[128,1024]{1,0:T(8,128)(2,1)S(1)} %collective-permute-done.11.refs_13_) | copy-start | bytes 786436
  86.1 30.7 %collective-permute-start.2 = (bf16[128,1024]{1,0:T(8,128)(2,1)}, bf16[128,1024]{1,0:T(8,128)(2,1)S(1)}, u32[]{:S(2)}, u32[]{:S(2)}) collective-permute-start(bf16[128,1024]{1,0:T(8,128)(2,1)} %get-tuple-element.36.refs_5_), channel_id=1, source_target_pairs={{0,1},{1,2},{2,3},{3,0},{4,5},{5,6},{6,7},{7,4},{8,9},{9,10},{10,1... | collective-permute-start | bytes 786440 | tf_op jit(solution)/shard_map/ppermute | solution.py:511
  89.0 80.2 %copy-start.2 = (bf16[128,1024]{1,0:T(8,128)(2,1)}, bf16[128,1024]{1,0:T(8,128)(2,1)S(1)}, u32[]{:S(2)}) copy-start(bf16[128,1024]{1,0:T(8,128)(2,1)S(1)} %collective-permute-done.6.refs_7_) | copy-start | bytes 786436
  89.0 40.0 %collective-permute-start.15 = (bf16[128,1024]{1,0:T(8,128)(2,1)}, bf16[128,1024]{1,0:T(8,128)(2,1)S(1)}, u32[]{:S(2)}, u32[]{:S(2)}) collective-permute-start(bf16[128,1024]{1,0:T(8,128)(2,1)} %get-tuple-element.37.refs_6_), channel_id=1, source_target_pairs={{0,1},{1,2},{2,3},{3,0},{4,5},{5,6},{6,7},{7,4},{8,9},{9,10},{10,1... | collective-permute-start | bytes 786440 | tf_op jit(solution)/shard_map/ppermute | solution.py:511
  92.7 76.6 %copy-start.3 = (bf16[128,1024]{1,0:T(8,128)(2,1)}, bf16[128,1024]{1,0:T(8,128)(2,1)S(1)}, u32[]{:S(2)}) copy-start(bf16[128,1024]{1,0:T(8,128)(2,1)S(1)} %collective-permute-done.12.refs_14_) | copy-start | bytes 786436
  92.7 42.7 %collective-permute-start.4 = (bf16[128,1024]{1,0:T(8,128)(2,1)}, bf16[128,1024]{1,0:T(8,128)(2,1)S(1)}, u32[]{:S(2)}, u32[]{:S(2)}) collective-permute-start(bf16[128,1024]{1,0:T(8,128)(2,1)} %get-tuple-element.37.refs_6_), channel_id=1, source_target_pairs={{0,3},{1,0},{2,1},{3,2},{4,7},{5,4},{6,5},{7,6},{8,11},{9,8},{10,9... | collective-permute-start | bytes 786440 | tf_op jit(solution)/shard_map/ppermute | solution.py:511
  94.7 74.6 %copy-start.1 = (bf16[128,1024]{1,0:T(8,128)(2,1)}, bf16[128,1024]{1,0:T(8,128)(2,1)S(1)}, u32[]{:S(2)}) copy-start(bf16[128,1024]{1,0:T(8,128)(2,1)S(1)} %collective-permute-done.7.refs_8_) | copy-start | bytes 786436
  94.7 42.0 %collective-permute-start.13 = (bf16[128,1024]{1,0:T(8,128)(2,1)S(1)}, bf16[128,1024]{1,0:T(8,128)(2,1)S(1)}, u32[]{:S(2)}, u32[]{:S(2)}) collective-permute-start(bf16[128,1024]{1,0:T(8,128)(2,1)S(1)} %copy-done.4), channel_id=1, source_target_pairs={{0,1},{1,2},{2,3},{3,0},{4,5},{5,6},{6,7},{7,4},{8,9},{9,10},{10,1... | collective-permute-start | bytes 786440 | tf_op jit(solution)/shard_map/ppermute | solution.py:511
  110.4 58.9 %copy-start.8 = (bf16[128,1024]{1,0:T(8,128)(2,1)}, bf16[128,1024]{1,0:T(8,128)(2,1)S(1)}, u32[]{:S(2)}) copy-start(bf16[128,1024]{1,0:T(8,128)(2,1)S(1)} %collective-permute-done.10.refs_11_) | copy-start | bytes 786436
  110.4 33.6 %collective-permute-start.8 = (bf16[128,1024]{1,0:T(8,128)(2,1)S(1)}, bf16[128,1024]{1,0:T(8,128)(2,1)S(1)}, u32[]{:S(2)}, u32[]{:S(2)}) collective-permute-start(bf16[128,1024]{1,0:T(8,128)(2,1)S(1)} %copy-done.4), channel_id=1, source_target_pairs={{0,3},{1,0},{2,1},{3,2},{4,7},{5,4},{6,5},{7,6},{8,11},{9,8},{10,9... | collective-permute-start | bytes 786440 | tf_op jit(solution)/shard_map/ppermute | solution.py:511
  116.8 52.5 %copy-start.6 = (bf16[128,1024]{1,0:T(8,128)(2,1)}, bf16[128,1024]{1,0:T(8,128)(2,1)S(1)}, u32[]{:S(2)}) copy-start(bf16[128,1024]{1,0:T(8,128)(2,1)S(1)} %collective-permute-done.2.refs_17_) | copy-start | bytes 786436
  116.8 34.3 %collective-permute-start.9 = (bf16[128,1024]{1,0:T(8,128)(2,1)S(1)}, bf16[128,1024]{1,0:T(8,128)(2,1)S(1)}, u32[]{:S(2)}, u32[]{:S(2)}) collective-permute-start(bf16[128,1024]{1,0:T(8,128)(2,1)S(1)} %copy-done.5), channel_id=1, source_target_pairs={{0,3},{1,0},{2,1},{3,2},{4,7},{5,4},{6,5},{7,6},{8,11},{9,8},{10,9... | collective-permute-start | bytes 786440 | tf_op jit(solution)/shard_map/ppermute | solution.py:511
  129.1 40.2 %copy-start.9 = (bf16[128,1024]{1,0:T(8,128)(2,1)}, bf16[128,1024]{1,0:T(8,128)(2,1)S(1)}, u32[]{:S(2)}) copy-start(bf16[128,1024]{1,0:T(8,128)(2,1)S(1)} %collective-permute-done.15.refs_18_) | copy-start | bytes 786436
  129.1 30.9 %collective-permute-start.14 = (bf16[128,1024]{1,0:T(8,128)(2,1)S(1)}, bf16[128,1024]{1,0:T(8,128)(2,1)S(1)}, u32[]{:S(2)}, u32[]{:S(2)}) collective-permute-start(bf16[128,1024]{1,0:T(8,128)(2,1)S(1)} %copy-done.5), channel_id=1, source_target_pairs={{0,1},{1,2},{2,3},{3,0},{4,5},{5,6},{6,7},{7,4},{8,9},{9,10},{10,1... | collective-permute-start | bytes 786440 | tf_op jit(solution)/shard_map/ppermute | solution.py:511
  135.4 33.9 %copy-start.7 = (bf16[128,1024]{1,0:T(8,128)(2,1)}, bf16[128,1024]{1,0:T(8,128)(2,1)S(1)}, u32[]{:S(2)}) copy-start(bf16[128,1024]{1,0:T(8,128)(2,1)S(1)} %collective-permute-done.4.refs_12_) | copy-start | bytes 786436
  135.4 30.2 %collective-permute-start.16 = (bf16[128,1024]{1,0:T(8,128)(2,1)S(1)}, bf16[128,1024]{1,0:T(8,128)(2,1)S(1)}, u32[]{:S(2)}, u32[]{:S(2)}) collective-permute-start(bf16[128,1024]{1,0:T(8,128)(2,1)S(1)} %collective-permute-done.11.refs_13_), channel_id=1, source_target_pairs={{0,1},{1,2},{2,3},{3,0},{4,5},{5,6},{6,7},{7,4},{8,9},{9,10},{10,1... | collective-permute-start | bytes 786440 | tf_op jit(solution)/shard_map/ppermute | solution.py:511
  136.7 32.6 %copy-start.10 = (bf16[128,1024]{1,0:T(8,128)(2,1)}, bf16[128,1024]{1,0:T(8,128)(2,1)S(1)}, u32[]{:S(2)}) copy-start(bf16[128,1024]{1,0:T(8,128)(2,1)S(1)} %collective-permute-done.13.refs_15_) | copy-start | bytes 786436
  136.7 49.3 %collective-permute-start.17 = (bf16[128,1024]{1,0:T(8,128)(2,1)S(1)}, bf16[128,1024]{1,0:T(8,128)(2,1)}, u32[]{:S(2)}, u32[]{:S(2)}) collective-permute-start(bf16[128,1024]{1,0:T(8,128)(2,1)S(1)} %collective-permute-done.7.refs_8_), channel_id=1, source_target_pairs={{0,3},{1,0},{2,1},{3,2},{4,7},{5,4},{6,5},{7,6},{8,11},{9,8},{10,9... | collective-permute-start | bytes 786440 | tf_op jit(solution)/shard_map/ppermute | solution.py:511
  143.9 25.4 %copy-start.12 = (bf16[128,1024]{1,0:T(8,128)(2,1)}, bf16[128,1024]{1,0:T(8,128)(2,1)S(1)}, u32[]{:S(2)}) copy-start(bf16[128,1024]{1,0:T(8,128)(2,1)S(1)} %collective-permute-done.8.refs_9_) | copy-start | bytes 786436
  143.9 42.1 %collective-permute-start.18 = (bf16[128,1024]{1,0:T(8,128)(2,1)S(1)}, bf16[128,1024]{1,0:T(8,128)(2,1)S(1)}, u32[]{:S(2)}, u32[]{:S(2)}) collective-permute-start(bf16[128,1024]{1,0:T(8,128)(2,1)S(1)} %collective-permute-done.13.refs_15_), channel_id=1, source_target_pairs={{0,1},{1,2},{2,3},{3,0},{4,5},{5,6},{6,7},{7,4},{8,9},{9,10},{10,1... | collective-permute-start | bytes 786440 | tf_op jit(solution)/shard_map/ppermute | solution.py:511
  151.1 18.2 %copy-start.11 = (bf16[128,1024]{1,0:T(8,128)(2,1)}, bf16[128,1024]{1,0:T(8,128)(2,1)S(1)}, u32[]{:S(2)}) copy-start(bf16[128,1024]{1,0:T(8,128)(2,1)S(1)} %collective-permute-done.9.refs_10_) | copy-start | bytes 786436
  151.1 35.0 %collective-permute-start.19 = (bf16[128,1024]{1,0:T(8,128)(2,1)S(1)}, bf16[128,1024]{1,0:T(8,128)(2,1)}, u32[]{:S(2)}, u32[]{:S(2)}) collective-permute-start(bf16[128,1024]{1,0:T(8,128)(2,1)S(1)} %collective-permute-done.9.refs_10_), channel_id=1, source_target_pairs={{0,3},{1,0},{2,1},{3,2},{4,7},{5,4},{6,5},{7,6},{8,11},{9,8},{10,9... | collective-permute-start | bytes 786440 | tf_op jit(solution)/shard_map/ppermute | solution.py:511
  159.9 5.6 %copy-start.14 = (bf16[128,1024]{1,0:T(8,128)(2,1)}, bf16[128,1024]{1,0:T(8,128)(2,1)S(1)}, u32[]{:S(2)}) copy-start(bf16[128,1024]{1,0:T(8,128)(2,1)S(1)} %collective-permute-done.14.refs_16_) | copy-start | bytes 786436
  159.9 34.2 %collective-permute-start.3 = (bf16[128,1024]{1,0:T(8,128)(2,1)S(1)}, bf16[128,1024]{1,0:T(8,128)(2,1)S(1)}, u32[]{:S(2)}, u32[]{:S(2)}) collective-permute-start(bf16[128,1024]{1,0:T(8,128)(2,1)S(1)} %collective-permute-done.2.refs_17_), channel_id=1, source_target_pairs={{0,1},{1,2},{2,3},{3,0},{4,5},{5,6},{6,7},{7,4},{8,9},{9,10},{10,1... | collective-permute-start | bytes 786440 | tf_op jit(solution)/shard_map/ppermute | solution.py:511
  165.6 0.7 copy-start.13
  166.3 27.9 %collective-permute-start.5 = (bf16[128,1024]{1,0:T(8,128)(2,1)S(1)}, bf16[128,1024]{1,0:T(8,128)(2,1)}, u32[]{:S(2)}, u32[]{:S(2)}) collective-permute-start(bf16[128,1024]{1,0:T(8,128)(2,1)S(1)} %collective-permute-done.4.refs_12_), channel_id=1, source_target_pairs={{0,3},{1,0},{2,1},{3,2},{4,7},{5,4},{6,5},{7,6},{8,11},{9,8},{10,9... | collective-permute-start | bytes 786440 | tf_op jit(solution)/shard_map/ppermute | solution.py:511
  186.0 0.7 copy-start.15
  194.2 0.7 copy-start.16
Sparse Core Ops, SparseCore 0:
  25.8 81.5 all-gather.2
